TPU v7x, 128 devices: a whole 4x4x4 slice. The times are simulated.
128 devices in a mesh: users: 128 (over y, z, x, core).
Axes of the slice: x: 4, y: 4, z: 4, core: 2. Of those that a mesh axis runs over, the one named last changes fastest.
Arguments:
- tile_owner: int32 [16384, 1], P('users'), may hold values from 0 to 127; in each aligned block of 128 rows (0 to 127, 128 to 255, ...) at most 2 rows name the same one
- tile_slot: int32 [16384], P('users'), may hold values from 0 to 15
- tile_cblock: int32 [16384], P('users'), may hold values from 0 to 63
- tile_context: int32 [16384, 512], P('users'), may hold values from 0 to 7
- tile_weights: bfloat16 [16384, 128, 512], P('users'), as said below
- item_factors: bfloat16 [2048, 64, 128], P('users'), may hold values from -0.5 to 0.5
- context_factors: bfloat16 [8, 512], replicated, may hold values from -0.5 to 0.5
- user_basis: float32 [65536, 128], P('users'), may hold values from -6 to 6
- user_counts: int32 [128], P('users'), may hold values from 256 to 512, as said below
Outputs:
- basis: float32 [65536, 128], P('users')
- core_out: float32 [128, 512], replicated
Inputs may be any that keep to these rules, and one draw needn't show every extreme that they name: `tile_owner`: among the 128 tiles of one device (aligned blocks of 128 rows), at most 2 name the same owner, and this is reached. `user_counts`: rows of a device at and beyond its count carry no events; some device has 512 live rows and some 512 // 2. tile_weights[t, :, u] is zero for u >= user_counts[t // 128].
All inputs are finite; a program needn't handle non-finite values.
Results may differ from a plain program's by a relative error of at most 0.006.
Values may be sent and summed in bfloat16 or wider, within the bound.
A program may use at most 128 MiB of HBM per device.

v0:
```python
import jax
import jax.numpy as jnp
from jax import lax
from jax.sharding import PartitionSpec as P

CB = 8
SLOTS = 2


HIGH = lax.Precision.HIGHEST


def cholesky_lower(gram_matrix):
    order = gram_matrix.shape[0]
    indices = jnp.arange(order, dtype=jnp.int32)

    def column_step(column, carry):
        remain, factor_low = carry
        marker = (indices == column).astype(jnp.float32)
        column_vals = jnp.dot(remain, marker, precision=HIGH)
        pivot = jnp.sqrt(jnp.dot(marker, column_vals, precision=HIGH))
        column_vals = jnp.where(indices >= column, column_vals / pivot, jnp.zeros_like(column_vals))
        remain = remain - column_vals[:, None] * column_vals[None, :]
        factor_low = factor_low + column_vals[:, None] * marker[None, :]
        return (remain, factor_low)

    start = (gram_matrix, jnp.zeros_like(gram_matrix))
    return lax.fori_loop(0, order, column_step, start)[1]


def inverse_lower(factor_low):
    order = factor_low.shape[0]
    indices = jnp.arange(order, dtype=jnp.int32)

    def row_step(row, inverse):
        marker = (indices == row).astype(jnp.float32)
        row_vals = jnp.dot(marker, factor_low, precision=HIGH)
        pivot = jnp.dot(row_vals, marker, precision=HIGH)
        new_row = (marker - jnp.dot(row_vals, inverse, precision=HIGH)) / pivot
        return inverse + marker[:, None] * new_row[None, :]

    return lax.fori_loop(0, order, row_step, jnp.zeros_like(factor_low))


def upper_of(gram_matrix):
    return cholesky_lower(gram_matrix).T


def body(
    tile_owner,
    tile_slot,
    tile_cblock,
    tile_context,
    tile_weights,
    item_factors,
    context_factors,
    user_basis,
    user_counts,
):
    devices = lax.axis_size("users")
    owners = tile_owner[:, 0]
    rank_c = context_factors.shape[0]
    rank_i = item_factors.shape[1]
    block_len = item_factors.shape[2]
    user_rows = tile_weights.shape[2]
    total_users = user_rows * devices
    ctx_block = tile_context.shape[0] * 0 + CB
    owner_hits = owners[:, None] == jnp.arange(devices, dtype=jnp.int32)[None, :]
    owner_ints = owner_hits.astype(jnp.int32)
    earlier = jnp.cumsum(owner_ints, axis=0) - owner_ints
    position = jnp.sum(earlier * owner_ints, axis=1)
    placed = owner_hits[:, :, None] & (
        position[:, None, None] == jnp.arange(SLOTS, dtype=jnp.int32)[None, None, :]
    )
    requests = jnp.sum(jnp.where(placed, tile_slot[:, None, None], 0), axis=0)
    found = item_factors[lax.all_to_all(requests, "users", split_axis=0, concat_axis=0, tiled=True)]
    fetched = lax.all_to_all(found, "users", split_axis=0, concat_axis=0, tiled=True)
    blocks = fetched.reshape(devices * SLOTS, rank_i, block_len)[owners * SLOTS + position]
    products = jnp.einsum(
        "tai,tiu->tau", blocks, tile_weights, preferred_element_type=jnp.float32
    ).astype(jnp.bfloat16)
    lookup = context_factors.astype(jnp.float32).reshape(rank_c, -1, ctx_block)
    chosen = (tile_cblock[:, None] == jnp.arange(lookup.shape[1], dtype=jnp.int32)[None, :]).astype(
        jnp.float32
    )
    block_values = jnp.einsum("rbk,tb->trk", lookup, chosen).astype(jnp.bfloat16)
    context_hits = (
        tile_context[:, None, :] == jnp.arange(ctx_block, dtype=jnp.int32)[None, :, None]
    ).astype(jnp.bfloat16)
    context_values = jnp.einsum(
        "trk,tku->tru", block_values, context_hits, preferred_element_type=jnp.float32
    ).astype(jnp.bfloat16)
    ytrans = jnp.einsum(
        "tru,tau->rau", context_values, products, preferred_element_type=jnp.float32
    )
    ytrans = ytrans.reshape(rank_c * rank_i, user_rows)
    living = jnp.arange(user_rows, dtype=jnp.int32) < user_counts[0]
    ytrans = jnp.where(living[None, :], ytrans, jnp.zeros_like(ytrans))
    local_projection = jnp.dot(ytrans, user_basis, precision=HIGH)
    scale_root = jnp.sqrt(jnp.float32(total_users))
    projection = lax.psum(local_projection, "users")
    projected = lax.dot_general(ytrans, projection, (((0,), (0,)), ((), ())), precision=HIGH)
    gram_matrix = lax.psum(jnp.dot(projected.T, projected, precision=HIGH), "users")
    inverse = inverse_lower(upper_of(gram_matrix).T)
    basis = jnp.dot(projected, inverse.T, precision=HIGH) * scale_root
    core_out = lax.psum(
        lax.dot_general(basis, ytrans, (((0,), (1,)), ((), ())), precision=HIGH), "users"
    ) / jnp.float32(total_users)
    return (basis, core_out)


def solution(mesh):
    return jax.shard_map(
        body,
        mesh=mesh,
        in_specs=(
            P("users", None),
            P("users"),
            P("users"),
            P("users", None),
            P("users", None, None),
            P("users", None, None),
            P(),
            P("users", None),
            P("users"),
        ),
        out_specs=(P("users", None), P()),
        check_vma=False,
    )
```

profile of v0, /device:TPU:1, one launch (start us, length us, event | category | flops | bytes accessed | tf_op | source)
XLA Modules:
  0.0 1281.7 jit_solution(113786225453500976)
XLA Ops:
  9.9 20.8 %all_to_all.17 = s32[128,1,2]{2,1,0:T(1,128)S(1)} all-to-all(s32[128,1,2]{2,1,0:T(1,128)S(1)} %copy.17), channel_id=1, replica_groups=mesh['users'=128] {'users'}, dimensions={0} | all-to-all | bytes 2048 | tf_op jit(solution)/shard_map/all_to_all | solution.py:76
  30.9 3.1 gather_fusion
  33.9 5.6 all-to-all-start.1
  40.7 2.0 copy.21
  43.4 48.8 %all-to-all-done.1 = bf16[128,2,64,128]{3,2,1,0:T(8,128)(2,1)} async-done(((bf16[128,2,64,128]{3,2,1,0:T(8,128)(2,1)}), bf16[128,2,64,128]{3,2,1,0:T(8,128)(2,1)}, u32[]{:S(2)}, u32[]{:S(2)}) %all-to-all-start.1) | async-done | bytes 4194336 | tf_op jit(solution)/shard_map/all_to_all | solution.py:77
  92.2 3.1 gather_fusion.1
  95.4 11.4 convolution_convert_fusion
  106.8 13.7 %copy.20 = bf16[128,64,512]{0,1,2:T(8,128)(2,1)} copy(bf16[128,64,512]{2,1,0:T(8,128)(2,1)} %convolution_convert_fusion) | data formatting | bytes 16777216 | tf_op jit(solution)/shard_map/convert_element_type | solution.py:81
  120.5 6.7 convolution_bitcast_fusion.2
  127.2 1.7 copy.22
  130.2 2.6 fusion.28
  133.1 139.5 %all-reduce.4.cloned.1.call-done = f32[512,128]{1,0:T(8,128)} async-done(((f32[512,128]{1,0:T(8,128)}), f32[512,128]{1,0:T(8,128)}) %all-reduce.4.cloned.1.call-update) | async-done | bytes 262160 | tf_op jit(solution)/shard_map/psum | solution.py:101
  272.6 2.8 fusion.29
  276.7 138.5 %all-reduce.6.cloned.1.call-done = f32[128,128]{1,0:T(8,128)} async-done(((f32[128,128]{1,0:T(8,128)}), f32[128,128]{1,0:T(8,128)}) %all-reduce.6.cloned.1.call-update) | async-done | bytes 65552 | tf_op jit(solution)/shard_map/psum | solution.py:103
  415.2 499.9 %while.32 = (s32[]{:T(128)}, f32[128,128]{1,0:T(8,128)}, f32[128,128]{1,0:T(8,128)S(1)}, s32[]{:T(128)}, s32[]{:T(128)}) while((s32[]{:T(128)}, f32[128,128]{1,0:T(8,128)}, f32[128,128]{1,0:T(8,128)S(1)}, s32[]{:T(128)}, s32[]{:T(128)}) %tuple.76), condition=%wide.region_6.7_spmd.clone.clone, body=%wide.region_5.6_spmd.clone.clone.sunk | while | flops 279682 | bytes 330851 | solution.py:28
  415.2 1.6 fusion.64
  419.1 1.6 fusion.64
  423.0 1.6 fusion.64
  426.9 1.6 fusion.64
  430.8 1.6 fusion.64
  915.1 215.8 %while.31 = (s32[]{:T(128)}, f32[128,128]{1,0:T(8,128)S(1)}, f32[128,128]{1,0:T(8,128)S(1)}, s32[]{:T(128)}, s32[]{:T(128)}) while((s32[]{:T(128)}, f32[128,128]{1,0:T(8,128)S(1)}, f32[128,128]{1,0:T(8,128)S(1)}, s32[]{:T(128)}, s32[]{:T(128)}) %tuple.79), condition=%wide.region_8.9_spmd.clone, body=%wide.region_7.8_spmd.clone.sunk | while | flops 460034 | bytes 265308 | solution.py:42
  1131.4 2.0 fusion.31
  1133.4 140.1 %all-reduce.8.cloned.1.call-done = f32[128,512]{1,0:T(8,128)} async-done(((f32[128,512]{1,0:T(8,128)}), f32[128,512]{1,0:T(8,128)}) %all-reduce.8.cloned.1.call-update) | async-done | bytes 262160 | tf_op jit(solution)/shard_map/psum | solution.py:106
  1273.5 1.7 broadcast_multiply_fusion
  (1061 shorter events, 619.7 us)
Async XLA Ops:
  7.2 23.7 %copy-start = (bf16[16,64,128]{2,1,0:T(8,128)(2,1)S(1)}, bf16[16,64,128]{2,1,0:T(8,128)(2,1)}, u32[]{:S(2)}) copy-start(bf16[16,64,128]{2,1,0:T(8,128)(2,1)} %param.18) | copy-start | bytes 786436
  33.9 5.6 copy-start.4
  33.9 5.9 copy-start.6
  33.9 6.3 copy-start.3
  33.9 58.3 %all-to-all-start.1 = ((bf16[128,2,64,128]{3,2,1,0:T(8,128)(2,1)}), bf16[128,2,64,128]{3,2,1,0:T(8,128)(2,1)}, u32[]{:S(2)}, u32[]{:S(2)}) async-start(bf16[128,2,64,128]{3,2,1,0:T(8,128)(2,1)} %bitcast.82), calls=%async_computation.1 | async-start | bytes 8388608 | tf_op jit(solution)/shard_map/all_to_all | solution.py:77
  39.5 3.8 copy-start.5
  39.5 233.1 %all-reduce.4.cloned.1.call-start = ((), (), s32[]{:S(2)}) async-start(), calls=%async_computation.2 | async-start | bytes 524288 | tf_op jit(solution)/shard_map/psum | solution.py:101
  106.8 13.7 %copy-start.1 = (bf16[128,8,512]{0,1,2:T(8,128)(2,1)S(1)}, bf16[128,8,512]{0,1,2:T(8,128)(2,1)}, u32[]{:S(2)}) copy-start(bf16[128,8,512]{0,1,2:T(8,128)(2,1)} %copy.21) | copy-start | bytes 3145732
  132.9 282.3 %all-reduce.6.cloned.1.call-start = ((), (), s32[]{:S(2)}) async-start(), calls=%async_computation.3 | async-start | bytes 131072 | tf_op jit(solution)/shard_map/psum | solution.py:103
  276.6 996.9 %all-reduce.8.cloned.1.call-start = ((), (), s32[]{:S(2)}) async-start(), calls=%async_computation.4 | async-start | bytes 524288 | tf_op jit(solution)/shard_map/psum | solution.py:106
  1131.4 143.8 %copy-start.2 = (f32[512,128]{1,0:T(8,128)}, f32[512,128]{1,0:T(8,128)S(1)}, u32[]{:S(2)}) copy-start(f32[512,128]{1,0:T(8,128)S(1)} %convolution_multiply_fusion) | copy-start | bytes 786436
Sparse Core Ops, SparseCore 0:
  133.0 139.5 all-reduce.3
  277.9 137.2 all-reduce.5
  1133.5 139.9 all-reduce.7
where the time goes:
time: 1300 us; the launch traced here: 1280 us
  waiting for transfers between devices  467 us (36%)
  matrix products  435 us (33%)
  other arithmetic  219 us (17%)
  loops' own time  95.2 us (7%)
  local copies, waits for them, and re-layouts  24.4 us (2%)
  blocking collectives  20.8 us (2%)
  between operations  14.6 us (1%)
    dot_general x128, matrix products, column_step(): column_vals = jnp.dot(remain, marker, precision=HIGH)  209 us
    add x128, other arithmetic, column_step(): factor_low = factor_low + column_vals[:, None] * marker[None, :]  198 us
    psum x1, waiting for transfers between devices, body(): lax.psum(lax.dot_general(basis, ytrans, (((0,), (1,)), ((), ())), precisi...  140 us
    psum x1, waiting for transfers between devices, body(): projection = lax.psum(local_projection, 'users')  139 us
    psum x1, waiting for transfers between devices, body(): lax.psum(jnp.dot(projected.T, projected, precision=HIGH), 'users')  139 us
    dot_general x128, matrix products, row_step(): new_row = (marker - jnp.dot(row_vals, inverse, precision=HIGH)) / pivot  102 us
    dot_general x128, matrix products, row_step(): row_vals = jnp.dot(marker, factor_low, precision=HIGH)  96.5 us
    another operation x1, loops' own time, cholesky_lower(): return lax.fori_loop(0, order, column_step, start)[1]  91.4 us
  transfers between devices with their start and end apart: 4, of which 4 were waited for; matrix products, arithmetic and copies ran while one was open for 0% of the time, Pallas kernels for 0%

commit v1 on v0

--- a/solution.py
+++ b/solution.py
@@ -1,49 +1,222 @@
+import functools
+
 import jax
 import jax.numpy as jnp
 from jax import lax
+from jax.experimental import pallas as pl
+from jax.experimental.pallas import tpu as pltpu
 from jax.sharding import PartitionSpec as P
 
+MESH = pl.DeviceIdType.MESH
+F32, BF16 = jnp.float32, jnp.bfloat16
+NN = (((1,), (0,)), ((), ()))
+NT = (((1,), (1,)), ((), ()))
+TN = (((0,), (0,)), ((), ()))
+BLOCKS = [(i, j) for i in range(4) for j in range(i, 4)]
+TILES = 224
+HALF, QUART, SIXT = 112, 28, 7
+PANEL = 16
 CB = 8
 SLOTS = 2
 
 
-HIGH = lax.Precision.HIGHEST
-
-
-def cholesky_lower(gram_matrix):
-    order = gram_matrix.shape[0]
-    indices = jnp.arange(order, dtype=jnp.int32)
-
-    def column_step(column, carry):
-        remain, factor_low = carry
-        marker = (indices == column).astype(jnp.float32)
-        column_vals = jnp.dot(remain, marker, precision=HIGH)
-        pivot = jnp.sqrt(jnp.dot(marker, column_vals, precision=HIGH))
-        column_vals = jnp.where(indices >= column, column_vals / pivot, jnp.zeros_like(column_vals))
-        remain = remain - column_vals[:, None] * column_vals[None, :]
-        factor_low = factor_low + column_vals[:, None] * marker[None, :]
-        return (remain, factor_low)
-
-    start = (gram_matrix, jnp.zeros_like(gram_matrix))
-    return lax.fori_loop(0, order, column_step, start)[1]
-
-
-def inverse_lower(factor_low):
-    order = factor_low.shape[0]
-    indices = jnp.arange(order, dtype=jnp.int32)
-
-    def row_step(row, inverse):
-        marker = (indices == row).astype(jnp.float32)
-        row_vals = jnp.dot(marker, factor_low, precision=HIGH)
-        pivot = jnp.dot(row_vals, marker, precision=HIGH)
-        new_row = (marker - jnp.dot(row_vals, inverse, precision=HIGH)) / pivot
-        return inverse + marker[:, None] * new_row[None, :]
-
-    return lax.fori_loop(0, order, row_step, jnp.zeros_like(factor_low))
-
-
-def upper_of(gram_matrix):
-    return cholesky_lower(gram_matrix).T
+def split(x):
+    high = x.astype(BF16)
+    return high, (x - high.astype(F32)).astype(BF16)
+
+
+def dot1(a, b, dims):
+    return lax.dot_general(a, b, dims, preferred_element_type=F32)
+
+
+def dot3(a, b, dims):
+    ah, al = split(a)
+    bh, bl = split(b)
+    return dot1(ah, bh, dims) + (dot1(ah, bl, dims) + dot1(al, bh, dims))
+
+
+def tail_kernel(users, yt_ref, u_ref, basis_ref, core_ref, yh, yl, part, halfr, half, r1, q, r2, s2, r3,
+                full, sfull, pfull, aug, send_sem, recv_sem):
+    me = lax.axis_index("users")
+    core = me % 2
+    x, z, y = (me // 2) % 4, (me // 8) % 4, me // 32
+    pos1 = x * (1 - core) + y * core
+    pos2 = y * (1 - core) + z * core
+    pos3 = z * (1 - core) + x * core
+    str1 = 2 * (1 - core) + 32 * core
+    str2 = 32 * (1 - core) + 8 * core
+    str3 = 8 * (1 - core) + 2 * core
+    partner = me + 1 - 2 * core
+
+    def peer(pos, stride, off):
+        there = (pos + off) % 4
+        return there, me + (there - pos) * stride
+
+    barrier = pltpu.get_barrier_semaphore()
+    pl.semaphore_signal(barrier, inc=1, device_id=(partner,), device_id_type=MESH)
+    for pos, stride in ((pos1, str1), (pos2, str2), (pos3, str3)):
+        for off in (1, 2, 3):
+            pl.semaphore_signal(barrier, inc=1, device_id=(peer(pos, stride, off)[1],), device_id_type=MESH)
+
+    yh[...], yl[...] = split(yt_ref[...])
+    uh, ul = split(u_ref[...])
+    b = 0
+    for i in range(4):
+        rows = pl.ds(i * 128, 128)
+        right = pl.ds(i * 128, 512 - i * 128)
+        ah, al = yh[rows, :], yl[rows, :]
+        s = dot1(ah, yh[right, :], NT) + (dot1(ah, yl[right, :], NT) + dot1(al, yh[right, :], NT))
+        for j in range(i, 4):
+            k = j - i
+            part[pl.ds(b * 16, 16)] = s[:, k * 128:(k + 1) * 128].reshape(16, 8, 128)
+            b += 1
+    for i in range(4):
+        rows = pl.ds(i * 128, 128)
+        ah, al = yh[rows, :], yl[rows, :]
+        p = dot1(ah, uh, NN) + (dot1(ah, ul, NN) + dot1(al, uh, NN))
+        part[pl.ds((10 + i) * 16, 16)] = p.reshape(16, 8, 128)
+
+    pl.semaphore_wait(barrier, 10)
+
+    def copy(src, dst, n, device):
+        return pltpu.make_async_remote_copy(src_ref=src, dst_ref=dst, send_sem=send_sem.at[n],
+                                            recv_sem=recv_sem.at[n], device_id=(device,), device_id_type=MESH)
+
+    c = copy(part.at[pl.ds((1 - core) * HALF, HALF)], halfr, 0, partner)
+    c.start()
+    c.wait()
+    half[...] = part[pl.ds(core * HALF, HALF)] + halfr[...]
+
+    copies = []
+    for off in (1, 2, 3):
+        there, device = peer(pos1, str1, off)
+        c = copy(half.at[pl.ds(there * QUART, QUART)], r1.at[off - 1], off, device)
+        c.start()
+        copies.append(c)
+    for c in copies:
+        c.wait()
+    q[...] = (half[pl.ds(pos1 * QUART, QUART)] + r1[0]) + (r1[1] + r1[2])
+
+    copies = []
+    for off in (1, 2, 3):
+        there, device = peer(pos2, str2, off)
+        c = copy(q.at[pl.ds(there * SIXT, SIXT)], r2.at[off - 1], 3 + off, device)
+        c.start()
+        copies.append(c)
+    for c in copies:
+        c.wait()
+    mine = (q[pl.ds(pos2 * SIXT, SIXT)] + r2[0]) + (r2[1] + r2[2])
+    s2[...] = mine
+
+    copies = []
+    for off in (1, 2, 3):
+        there, device = peer(pos3, str3, off)
+        c = copy(s2, r3.at[pos3], 6 + off, device)
+        c.start()
+        copies.append(c)
+    r3[pos3] = mine
+    for c in copies:
+        c.wait()
+    at2 = core * HALF + pos1 * QUART + pos2 * SIXT
+    full[pl.ds(at2, SIXT)] = (r3[0] + r3[1]) + (r3[2] + r3[3])
+
+    copies = []
+    for off in (1, 2, 3):
+        there, device = peer(pos2, str2, off)
+        c = copy(full.at[pl.ds(at2, SIXT)], full.at[pl.ds(at2, SIXT)], 9 + off, device)
+        c.start()
+        copies.append(c)
+    for c in copies:
+        c.wait()
+    at1 = core * HALF + pos1 * QUART
+    copies = []
+    for off in (1, 2, 3):
+        there, device = peer(pos1, str1, off)
+        c = copy(full.at[pl.ds(at1, QUART)], full.at[pl.ds(at1, QUART)], 12 + off, device)
+        c.start()
+        copies.append(c)
+    for c in copies:
+        c.wait()
+    c = copy(full.at[pl.ds(core * HALF, HALF)], full.at[pl.ds(core * HALF, HALF)], 16, partner)
+    c.start()
+    c.wait()
+
+    for b, (i, j) in enumerate(BLOCKS):
+        blk = full[pl.ds(b * 16, 16)].reshape(128, 128)
+        sfull[pl.ds(i * 128, 128), pl.ds(j * 128, 128)] = blk
+        if i < j:
+            sfull[pl.ds(j * 128, 128), pl.ds(i * 128, 128)] = blk.T
+    for i in range(4):
+        pfull[pl.ds(i * 128, 128), :] = full[pl.ds((10 + i) * 16, 16)].reshape(128, 128)
+    p = pfull[...]
+    t = dot3(p.T, sfull[...], NN)
+    g = dot3(t, p, NN)
+    linv = cholesky_inverse(g, aug)
+    scale = float(users) ** 0.5
+    core_ref[...] = dot3(linv, t, NN) * (scale / users)
+    m = dot3(p, linv, NT) * scale
+    mh, ml = split(m)
+    basis_ref[...] = dot1(yh[...], mh, TN) + (dot1(yh[...], ml, TN) + dot1(yl[...], mh, TN))
+
+
+def cholesky_inverse(g, aug):
+    n = g.shape[0]
+    r0 = lax.broadcasted_iota(jnp.int32, (n, n), 0)
+    c0 = lax.broadcasted_iota(jnp.int32, (n, n), 1)
+    aug[:, pl.ds(0, n)] = g
+    aug[:, pl.ds(n, n)] = (r0 == c0).astype(F32)
+    sub = lax.broadcasted_iota(jnp.int32, (PANEL, n), 0)
+    for k in range(0, n, PANEL):
+        left = aug[pl.ds(k, PANEL), pl.ds(0, n)]
+        right = aug[pl.ds(k, PANEL), pl.ds(n, n)]
+        for j in range(PANEL):
+            col = jnp.broadcast_to(left[:, k + j:k + j + 1], (PANEL, n))
+            root = lax.rsqrt(col[j:j + 1, :])
+            lrow = left[j:j + 1, :] * root
+            rrow = right[j:j + 1, :] * root
+            mult = jnp.where(sub > j, col * root, 0.0)
+            left = jnp.where(sub == j, lrow, left - mult * lrow)
+            right = jnp.where(sub == j, rrow, right - mult * rrow)
+        aug[pl.ds(k, PANEL), pl.ds(n, n)] = right
+        if k + PANEL < n:
+            below = n - k - PANEL
+            rest = pl.ds(k + PANEL, below)
+            lh, ll = split(left)
+            rh, rl = split(right)
+            th, tl = lh[:, k + PANEL:], ll[:, k + PANEL:]
+            aug[rest, pl.ds(0, n)] -= dot1(th, lh, TN) + (dot1(th, ll, TN) + dot1(tl, lh, TN))
+            aug[rest, pl.ds(n, n)] -= dot1(th, rh, TN) + (dot1(th, rl, TN) + dot1(tl, rh, TN))
+    return aug[:, pl.ds(n, n)]
+
+
+def tail(yt, user_basis, users):
+    vm = pl.BlockSpec(memory_space=pltpu.VMEM)
+    return pl.pallas_call(
+        functools.partial(tail_kernel, users),
+        out_shape=(jax.ShapeDtypeStruct((512, 128), F32), jax.ShapeDtypeStruct((128, 512), F32)),
+        in_specs=[vm, vm],
+        out_specs=(vm, vm),
+        scratch_shapes=[
+            pltpu.VMEM((512, 512), BF16),
+            pltpu.VMEM((512, 512), BF16),
+            pltpu.VMEM((TILES, 8, 128), F32),
+            pltpu.VMEM((HALF, 8, 128), F32),
+            pltpu.VMEM((HALF, 8, 128), F32),
+            pltpu.VMEM((3, QUART, 8, 128), F32),
+            pltpu.VMEM((QUART, 8, 128), F32),
+            pltpu.VMEM((3, SIXT, 8, 128), F32),
+            pltpu.VMEM((SIXT, 8, 128), F32),
+            pltpu.VMEM((4, SIXT, 8, 128), F32),
+            pltpu.VMEM((TILES, 8, 128), F32),
+            pltpu.VMEM((512, 512), F32),
+            pltpu.VMEM((512, 128), F32),
+            pltpu.VMEM((128, 256), F32),
+            pltpu.SemaphoreType.DMA((17,)),
+            pltpu.SemaphoreType.DMA((17,)),
+        ],
+        compiler_params=pltpu.CompilerParams(collective_id=0, has_side_effects=True),
+        name="tail",
+    )(yt, user_basis)
 
 
 def body(
@@ -96,16 +269,7 @@
     ytrans = ytrans.reshape(rank_c * rank_i, user_rows)
     living = jnp.arange(user_rows, dtype=jnp.int32) < user_counts[0]
     ytrans = jnp.where(living[None, :], ytrans, jnp.zeros_like(ytrans))
-    local_projection = jnp.dot(ytrans, user_basis, precision=HIGH)
-    scale_root = jnp.sqrt(jnp.float32(total_users))
-    projection = lax.psum(local_projection, "users")
-    projected = lax.dot_general(ytrans, projection, (((0,), (0,)), ((), ())), precision=HIGH)
-    gram_matrix = lax.psum(jnp.dot(projected.T, projected, precision=HIGH), "users")
-    inverse = inverse_lower(upper_of(gram_matrix).T)
-    basis = jnp.dot(projected, inverse.T, precision=HIGH) * scale_root
-    core_out = lax.psum(
-        lax.dot_general(basis, ytrans, (((0,), (1,)), ((), ())), precision=HIGH), "users"
-    ) / jnp.float32(total_users)
+    basis, core_out = tail(ytrans, user_basis, total_users)
     return (basis, core_out)
 
 

time: 1300 us -> 172 us (0.13); the launches traced: 1280 us -> 171 us
  waiting for transfers between devices: 467 us -> 49.6 us
  matrix products: 435 us -> 18.7 us
  other arithmetic: 219 us -> 3.72 us
  loops' own time: 95.2 us -> 0 us
  Pallas kernels: 0 us -> 45.2 us
  between operations: 14.6 us -> 1.45 us
    psum x3 -> x0, waiting for transfers between devices: 418 us -> none  [the longest x1 140 us: body(): lax.psum(lax.dot_general(basis, ytrans, (((0,), (1,)), ((), ())), precisi...]
    dot_general x389 -> x0, matrix products: 417 us -> none  [the longest x128 209 us: column_step(): column_vals = jnp.dot(remain, marker, precision=HIGH)]
    add x256 -> x0, other arithmetic: 211 us -> none  [the longest x128 198 us: column_step(): factor_low = factor_low + column_vals[:, None] * marker[None, :]]
    another operation x2 -> x0, loops' own time: 95.2 us -> none  [the longest x1 91.4 us: cholesky_lower(): return lax.fori_loop(0, order, column_step, start)[1]]
    pallas_call x0 -> x1, Pallas kernels: none -> 45.2 us  [tail(): pl.pallas_call(functools.partial(tail_kernel, users), out_shape=(jax.Shap...]
  transfers between devices with their start and end apart: 4 -> 1, of which waited for: 4 -> 1; matrix products, arithmetic and copies ran while one was open for 0% -> 1% of each run, Pallas kernels for 0% -> 0%
where the time goes in v1:
time: 172 us; the launch traced here: 171 us
  waiting for transfers between devices  49.6 us (29%)
  Pallas kernels  45.2 us (26%)
  local copies, waits for them, and re-layouts  26 us (15%)
  blocking collectives  20.8 us (12%)
  matrix products  18.7 us (11%)
  starting transfers between devices  5.57 us (3%)
  other arithmetic  3.72 us (2%)
    all_to_all x1, waiting for transfers between devices, body(): lax.all_to_all(found, 'users', split_axis=0, concat_axis=0, tiled=True)  49.6 us
    pallas_call x1, Pallas kernels, tail(): pl.pallas_call(functools.partial(tail_kernel, users), out_shape=(jax.Shap...  45.2 us
    all_to_all x1, blocking collectives, body(): lax.all_to_all(requests, 'users', split_axis=0, concat_axis=0, tiled=True)  20.8 us
    convert_element_type x1, local copies, waits for them, and re-layouts, body(): products = jnp.einsum('tai,tiu->tau', blocks, tile_weights, preferred_ele...  13.7 us
    dot_general x1, matrix products, body(): jnp.einsum('tai,tiu->tau', blocks, tile_weights, preferred_element_type=j...  11.4 us
    dot_general x1, matrix products, body(): jnp.einsum('tru,tau->rau', context_values, products, preferred_element_ty...  6.7 us
    all_to_all x1, starting transfers between devices, body(): lax.all_to_all(found, 'users', split_axis=0, concat_axis=0, tiled=True)  5.57 us
  transfers between devices with their start and end apart: 1, of which 1 were waited for; matrix products, arithmetic and copies ran while one was open for 1% of the time, Pallas kernels for 0%

profile of v1, /device:TPU:1, one launch (start us, length us, event | category | flops | bytes accessed | tf_op | source)
XLA Modules:
  0.0 171.0 jit_solution(9358223504238746672)
XLA Ops:
  0.6 0.8 iota_compare_fusion.4
  1.4 0.2 reduce_window_sum.11
  1.6 0.8 select_reduce_fusion.1
  2.4 0.8 select_reduce_fusion
  3.2 0.1 copy.18
  3.4 20.8 %all_to_all.17 = s32[128,1,2]{2,1,0:T(1,128)S(1)} all-to-all(s32[128,1,2]{2,1,0:T(1,128)S(1)} %copy.18), channel_id=1, replica_groups=mesh['users'=128] {'users'}, dimensions={0} | all-to-all | bytes 2048 | tf_op jit(solution)/shard_map/all_to_all | solution.py:249
  24.2 0.1 reshape.99
  24.3 3.1 %gather_fusion = bf16[256,64,128]{2,1,0:T(8,128)(2,1)} fusion(bf16[16,64,128]{2,1,0:T(8,128)(2,1)S(1)} %copy-done, s32[1024]{0:T(1024)S(1)} %pad_clamp_fusion.1), kind=kCustom, calls=%fused_computation | custom fusion | bytes 8389632 | tf_op jit(solution)/shard_map/gather | solution.py:249
  27.4 5.6 %all-to-all-start.1 = ((bf16[128,2,64,128]{3,2,1,0:T(8,128)(2,1)}), bf16[128,2,64,128]{3,2,1,0:T(8,128)(2,1)}, u32[]{:S(2)}, u32[]{:S(2)}) async-start(bf16[128,2,64,128]{3,2,1,0:T(8,128)(2,1)} %bitcast.33), calls=%async_computation.1 | async-start | bytes 8388608 | tf_op jit(solution)/shard_map/all_to_all | solution.py:250
  33.0 0.2 reshape.95
  33.3 0.1 fusion.2
  33.4 0.2 copy.20
  33.7 0.4 fusion.1
  34.1 1.3 copy.22
  36.1 49.6 %all-to-all-done.1 = bf16[128,2,64,128]{3,2,1,0:T(8,128)(2,1)} async-done(((bf16[128,2,64,128]{3,2,1,0:T(8,128)(2,1)}), bf16[128,2,64,128]{3,2,1,0:T(8,128)(2,1)}, u32[]{:S(2)}, u32[]{:S(2)}) %all-to-all-start.1) | async-done | bytes 4194336 | tf_op jit(solution)/shard_map/all_to_all | solution.py:250
  85.7 3.1 %gather_fusion.1 = bf16[128,64,128]{2,1,0:T(8,128)(2,1)S(1)} fusion(bf16[256,64,128]{2,1,0:T(8,128)(2,1)} %bitcast.5, s32[1024]{0:T(1024)S(1)} %pad_clamp_fusion), kind=kCustom, calls=%fused_computation.1 | custom fusion | bytes 4194816 | tf_op jit(solution)/shard_map/gather | solution.py:251
  88.8 11.4 %convolution_convert_fusion = bf16[128,64,512]{2,1,0:T(8,128)(2,1)} fusion(bf16[128,64,128]{2,1,0:T(8,128)(2,1)S(1)} %gather_fusion.1, bf16[128,128,512]{2,1,0:T(8,128)(2,1)} %param.13), kind=kOutput, calls=%fused_computation.2 | convolution fusion | flops 1077936128 | bytes 27262976 | tf_op jit(solution)/shard_map/tai,tiu->tau/dot_general | solution.py:252
  100.2 13.7 %copy.21 = bf16[128,64,512]{0,1,2:T(8,128)(2,1)} copy(bf16[128,64,512]{2,1,0:T(8,128)(2,1)} %convolution_convert_fusion) | data formatting | bytes 16777216 | tf_op jit(solution)/shard_map/convert_element_type | solution.py:254
  113.9 6.7 %convolution_bitcast_fusion = f32[8,64,512]{1,0,2:T(8,128)S(1)} fusion(bf16[128,64,512]{0,1,2:T(8,128)(2,1)} %copy.21, bf16[128,8,512]{0,1,2:T(8,128)(2,1)S(1)} %copy.22), kind=kOutput, calls=%fused_computation.5 | convolution fusion | flops 67108864 | bytes 10485760 | tf_op jit(solution)/shard_map/tru,tau->rau/dot_general | solution.py:266
  120.6 0.7 copy.23
  121.3 1.1 bitcast_select_fusion.yt_ref
  122.4 45.2 %tail.1 = (f32[512,128]{1,0:T(8,128)}, f32[128,512]{1,0:T(8,128)}) custom-call(f32[512,512]{1,0:T(8,128)} %bitcast_select_fusion.yt_ref, f32[512,128]{1,0:T(8,128)} %u_ref.1), custom_call_target="tpu_custom_call" | custom-call | tf_op jit(solution)/shard_map/tail/pallas_call | solution.py:194
  167.7 1.7 copy.27
  169.3 1.7 copy.28
  (17 shorter events, 0.2 us)
Async XLA Ops:
  0.6 23.7 %copy-start = (bf16[16,64,128]{2,1,0:T(8,128)(2,1)S(1)}, bf16[16,64,128]{2,1,0:T(8,128)(2,1)}, u32[]{:S(2)}) copy-start(bf16[16,64,128]{2,1,0:T(8,128)(2,1)} %param.14) | copy-start | bytes 786436
  27.4 5.6 %copy-start.2 = (bf16[8,512]{1,0:T(8,128)(2,1)S(1)}, bf16[8,512]{1,0:T(8,128)(2,1)}, u32[]{:S(2)}) copy-start(bf16[8,512]{1,0:T(8,128)(2,1)} %param.15) | copy-start | bytes 24580
  27.4 5.9 %copy-start.4 = (s32[128]{0:T(128)S(1)}, s32[128]{0:T(128)}, u32[]{:S(2)}) copy-start(s32[128]{0:T(128)} %param.11) | copy-start | bytes 1540
  27.4 6.2 %copy-start.1 = (s32[128,512]{1,0:T(8,128)S(1)}, s32[128,512]{1,0:T(8,128)}, u32[]{:S(2)}) copy-start(s32[128,512]{1,0:T(8,128)} %param.12) | copy-start | bytes 786436
  27.4 58.3 %all-to-all-start.1 = ((bf16[128,2,64,128]{3,2,1,0:T(8,128)(2,1)}), bf16[128,2,64,128]{3,2,1,0:T(8,128)(2,1)}, u32[]{:S(2)}, u32[]{:S(2)}) async-start(bf16[128,2,64,128]{3,2,1,0:T(8,128)(2,1)} %bitcast.33), calls=%async_computation.1 | async-start | bytes 8388608 | tf_op jit(solution)/shard_map/all_to_all | solution.py:250
  33.0 3.1 %copy-start.3 = (s32[128,1]{0,1:T(1,128)S(1)}, s32[128,1]{0,1:T(1,128)}, u32[]{:S(2)}) copy-start(s32[128,1]{0,1:T(1,128)} %param.9) | copy-start | bytes 1540
